TPU v7x, 128 devices: a whole 4x4x4 slice. The times are simulated.
128 devices in a mesh: blk: 8 (over z_lo, x), head: 16 (over y, z_hi, core).
Axes of the slice: x: 4, y: 4, z: 4 (z_hi: 2, z_lo: 2; z = z_hi * 2 + z_lo), core: 2. Of those that a mesh axis runs over, the one named last changes fastest.
Arguments:
- qkv: bfloat16 [32768, 6144], P(('blk', 'head')), may hold values from -12 to 12
Outputs:
- attended: bfloat16 [32768, 2048], P(('blk', 'head'))
All inputs are finite; a program needn't handle non-finite values.
Results may differ from a plain program's by a relative error of at most 0.0059.
Values may be sent and summed in bfloat16 or wider, within the bound.
A program may use at most 128 MiB of HBM per device.

v0:
```python
import jax
import jax.numpy as jnp
from jax import lax
from jax.sharding import PartitionSpec as P

HEAD_DIM = 64
BLOCK = 2048
BLK_DEV = 2


def attend(query, pair):
    keys = pair[:, 0]
    values = pair[:, 1]
    tile = min(512, BLOCK)
    scale = HEAD_DIM ** (-0.5)

    def one_tile(query_tile):
        scores = (
            jnp.einsum("qhd,khd->hqk", query_tile, keys, preferred_element_type=jnp.float32) * scale
        )
        row_max = jnp.max(scores, axis=-1)
        probs = jnp.exp(scores - row_max[..., None]).astype(jnp.bfloat16)
        total = jnp.sum(probs.astype(jnp.float32), axis=-1)
        weighted = jnp.einsum("hqk,khd->hqd", probs, values, preferred_element_type=jnp.float32)
        return (row_max, total, weighted)

    tiles = query.reshape(BLOCK // tile, tile, query.shape[1], query.shape[2])
    return lax.map(one_tile, tiles)


def combine(partials):
    overall = partials[0][0]
    for entry in partials[1:]:
        overall = jnp.maximum(overall, entry[0])
    numer = jnp.zeros_like(partials[0][2])
    denom = jnp.zeros_like(partials[0][1])
    for row_max, total, weighted in partials:
        factor = jnp.exp(row_max - overall)
        numer = numer + factor[..., None] * weighted
        denom = denom + factor * total
    result = numer / denom[..., None]
    return result.transpose(0, 2, 1, 3).reshape(BLOCK, result.shape[1] * result.shape[3])


def on_device(qkv):
    rows = qkv.shape[0]
    heads_cols = qkv.shape[1] // 3
    shaped = qkv.reshape(rows, 3, heads_cols)
    grouped = lax.all_to_all(shaped, "head", split_axis=2, concat_axis=0, tiled=True)
    local_cols = grouped.shape[2]
    heads_here = local_cols // HEAD_DIM
    grid = grouped.reshape(BLK_DEV, BLOCK, 3, heads_here, HEAD_DIM)
    queries = grid[:, :, 0]
    pairs = grid[:, :, 1:3]
    device_bits = lax.axis_size("blk").bit_length() - 1
    partials = [[] for j in range(BLK_DEV)]

    def own_blocks():
        for j in range(BLK_DEV):
            partials[j].append(attend(queries[j], pairs[j]))
            partials[j].append(attend(queries[j], pairs[j ^ 1 << 0]))

    gathered = lax.all_gather(pairs, "blk", axis=0, tiled=True)
    mine = lax.axis_index("blk")
    for bit in range(device_bits):
        for j in range(BLK_DEV):
            where = jnp.bitwise_xor(mine, 1 << bit) * BLK_DEV + j
            chosen = lax.dynamic_index_in_dim(gathered, where, 0, keepdims=False)
            partials[j].append(attend(queries[j], chosen))
    own_blocks()
    outputs = jnp.concatenate([combine(partials[j]) for j in range(BLK_DEV)], axis=0).astype(
        jnp.bfloat16
    )
    return lax.all_to_all(outputs, "head", split_axis=0, concat_axis=1, tiled=True)


def solution(mesh):
    in_specs = (P(("blk", "head"), None),)
    out_specs = P(("blk", "head"), None)
    return jax.shard_map(
        on_device, mesh=mesh, in_specs=in_specs, out_specs=out_specs, check_vma=False
    )
```

profile of v0, /device:TPU:1, one launch (start us, length us, event | category | flops | bytes accessed | tf_op | source)
XLA Modules:
  0.0 471.0 jit_solution(7720879860149030022)
XLA Ops:
  6.5 3.2 copy.39
  9.7 17.2 %copy.40 = bf16[256,3,2048]{0,1,2:T(4,128)(2,1)} copy(bf16[256,3,2048]{0,2,1:T(8,128)(2,1)S(1)} %bitcast.366) | data formatting | bytes 6291456 | tf_op jit(solution)/shard_map/reshape | solution.py:48
  26.9 9.3 %all-to-all-start = ((bf16[256,3,2048]{0,1,2:T(4,128)(2,1)}), bf16[256,3,2048]{0,1,2:T(4,128)(2,1)}, u32[]{:S(2)}, u32[]{:S(2)}) async-start(bf16[256,3,2048]{0,1,2:T(4,128)(2,1)} %copy.40), calls=%async_computation | async-start | bytes 8388608 | tf_op jit(solution)/shard_map/all_to_all | solution.py:49
  36.2 52.6 %all-to-all-done = bf16[256,3,2048]{0,1,2:T(4,128)(2,1)} async-done(((bf16[256,3,2048]{0,1,2:T(4,128)(2,1)}), bf16[256,3,2048]{0,1,2:T(4,128)(2,1)}, u32[]{:S(2)}, u32[]{:S(2)}) %all-to-all-start) | async-done | bytes 3145760 | tf_op jit(solution)/shard_map/all_to_all | solution.py:49
  91.5 3.5 copy.42
  95.0 3.9 reshape.47
  100.8 5.2 %slice_reduce_fusion.1 = (bf16[2048,2,64]{0,2,1:T(8,128)(2,1)}, bf16[2048,2,64]{0,2,1:T(8,128)(2,1)}) fusion(bf16[2,2048,3,2,64]{1,0,4,3,2:T(2,128)(2,1)S(1)} %reshape.47), kind=kLoop, calls=%fused_computation.121 | loop fusion | bytes 2097152 | tf_op jit(solution)/shard_map/slice | solution.py:69
  106.0 4.2 fusion.62
  114.7 2.9 copy_bitcast_fusion
  118.9 21.6 %while.143 = (s32[]{:T(128)}, f32[4,2,512]{2,1,0:T(2,128)S(1)}, f32[4,2,512]{2,1,0:T(2,128)S(1)}, f32[4,2,512,64]{2,3,1,0:T(8,128)}, bf16[4,512,2,64]{1,3,2,0:T(...) while((s32[]{:T(128)}, f32[4,2,512]{2,1,0:T(2,128)S(1)}, ...), condition=%wide.region_15.16_spmd, body=%wide.region_12.15_spmd.sunk | while | flops 557840384 | bytes 26640988 | solution.py:28
  141.7 21.9 %while.144 = (s32[]{:T(128)}, f32[4,2,512]{2,1,0:T(2,128)S(1)}, f32[4,2,512]{2,1,0:T(2,128)S(1)}, f32[4,2,512,64]{2,3,1,0:T(8,128)}, bf16[4,512,2,64]{1,3,2,0:T(...) while((s32[]{:T(128)}, f32[4,2,512]{2,1,0:T(2,128)S(1)}, ...), condition=%wide.region_19.20_spmd, body=%wide.region_16.19_spmd.sunk | while | flops 557840384 | bytes 26640988 | solution.py:28
  164.7 21.6 %while.148 = (s32[]{:T(128)}, f32[4,2,512]{2,1,0:T(2,128)S(1)}, f32[4,2,512]{2,1,0:T(2,128)S(1)}, f32[4,2,512,64]{2,3,1,0:T(8,128)}, bf16[4,512,2,64]{1,3,2,0:T(...) while((s32[]{:T(128)}, f32[4,2,512]{2,1,0:T(2,128)S(1)}, ...), condition=%wide.region_35.36_spmd, body=%wide.region_32.35_spmd.sunk | while | flops 557840384 | bytes 26640988 | solution.py:28
  186.9 19.9 %while.149 = (s32[]{:T(128)}, f32[4,2,512]{2,1,0:T(2,128)S(1)}, f32[4,2,512]{2,1,0:T(2,128)S(1)}, f32[4,2,512,64]{2,3,1,0:T(8,128)S(1)}, bf16[4,512,2,64]{1,3,2,...) while((s32[]{:T(128)}, f32[4,2,512]{2,1,0:T(2,128)S(1)}, ...), condition=%wide.region_39.40_spmd, body=%wide.region_36.39_spmd.sunk | while | flops 557840384 | bytes 26640480 | solution.py:28
  206.8 83.2 %all-gather.2.cloned.1.call-done = bf16[16,2048,2,2,64]{1,4,3,2,0:T(8,128)(2,1)} async-done(((bf16[2,2048,2,2,64]{1,4,3,2,0:T(8,128)(2,1)}), bf16[16,2048,2,2,64]{1,4,3,2,0:T(8,128)(2,1)}) %all-gather.2.cloned.1.call-update) | async-done | bytes 16777232 | tf_op jit(solution)/shard_map/all_gather | solution.py:63
  290.1 5.3 %dynamic-slice_bitcast_fusion.5 = (bf16[2048,2,2,64]{0,3,2,1:T(8,128)(2,1)S(1)}, bf16[2048,2,2,64]{0,3,2,1:T(8,128)(2,1)}, bf16[2048,2,2,64]{0,3,2,1:T(8,128)(2,...) fusion(bf16[16,2048,2,2,64]{1,4,3,2,0:T(8,128)(2,1)} %all-gather.2., ...), kind=kLoop, calls=%fused_computation.132 | loop fusion | bytes 12582936 | tf_op jit(solution)/shard_map/jit(dynamic_index_in_dim)/squeeze | solution.py:68
  296.9 22.0 %while.140 = (s32[]{:T(128)}, f32[4,2,512]{2,1,0:T(2,128)S(1)}, f32[4,2,512]{2,1,0:T(2,128)S(1)}, f32[4,2,512,64]{2,3,1,0:T(8,128)}, bf16[4,512,2,64]{1,3,2,0:T(...) while((s32[]{:T(128)}, f32[4,2,512]{2,1,0:T(2,128)S(1)}, ...), condition=%wide.region_3.4_spmd, body=%wide.region_0.3_spmd.sunk | while | flops 557840384 | bytes 26640988 | solution.py:28
  319.1 19.9 %while.141 = (s32[]{:T(128)}, f32[4,2,512]{2,1,0:T(2,128)S(1)}, f32[4,2,512]{2,1,0:T(2,128)S(1)}, f32[4,2,512,64]{2,3,1,0:T(8,128)S(1)}, bf16[4,512,2,64]{1,3,2,...) while((s32[]{:T(128)}, f32[4,2,512]{2,1,0:T(2,128)S(1)}, ...), condition=%wide.region_7.8_spmd, body=%wide.region_4.7_spmd.sunk | while | flops 557840384 | bytes 26640480 | solution.py:28
  342.8 21.6 %while.142 = (s32[]{:T(128)}, f32[4,2,512]{2,1,0:T(2,128)S(1)}, f32[4,2,512]{2,1,0:T(2,128)S(1)}, f32[4,2,512,64]{2,3,1,0:T(8,128)}, bf16[4,512,2,64]{1,3,2,0:T(...) while((s32[]{:T(128)}, f32[4,2,512]{2,1,0:T(2,128)S(1)}, ...), condition=%wide.region_11.12_spmd, body=%wide.region_8.11_spmd.sunk | while | flops 557840384 | bytes 26640988 | solution.py:28
  364.4 3.2 fusion.60
  368.3 20.1 %while.145 = (s32[]{:T(128)}, f32[4,2,512]{2,1,0:T(2,128)S(1)}, f32[4,2,512]{2,1,0:T(2,128)S(1)}, f32[4,2,512,64]{2,3,1,0:T(8,128)S(1)}, bf16[4,512,2,64]{1,3,2,...) while((s32[]{:T(128)}, f32[4,2,512]{2,1,0:T(2,128)S(1)}, ...), condition=%wide.region_23.24_spmd, body=%wide.region_20.23_spmd.sunk | while | flops 557840384 | bytes 26640480 | solution.py:28
  392.2 21.6 %while.146 = (s32[]{:T(128)}, f32[4,2,512]{2,1,0:T(2,128)S(1)}, f32[4,2,512]{2,1,0:T(2,128)S(1)}, f32[4,2,512,64]{2,3,1,0:T(8,128)}, bf16[4,512,2,64]{1,3,2,0:T(...) while((s32[]{:T(128)}, f32[4,2,512]{2,1,0:T(2,128)S(1)}, ...), condition=%wide.region_27.28_spmd, body=%wide.region_24.27_spmd.sunk | while | flops 557840384 | bytes 26640988 | solution.py:28
  414.0 19.9 %while.147 = (s32[]{:T(128)}, f32[4,2,512]{2,1,0:T(2,128)S(1)}, f32[4,2,512]{2,1,0:T(2,128)S(1)}, f32[4,2,512,64]{2,3,1,0:T(8,128)S(1)}, bf16[4,512,2,64]{1,3,2,...) while((s32[]{:T(128)}, f32[4,2,512]{2,1,0:T(2,128)S(1)}, ...), condition=%wide.region_31.32_spmd, body=%wide.region_28.31_spmd.sunk | while | flops 557840384 | bytes 26640480 | solution.py:28
  434.0 2.9 fusion.61
  438.2 23.8 %all_to_all.31 = bf16[16,256,128]{2,1,0:T(8,128)(2,1)S(1)} all-to-all(bf16[16,256,128]{2,1,0:T(8,128)(2,1)S(1)} %bitcast.367), channel_id=1, replica_groups=mesh['blk'=8,'head'=16] {'head'}, dimensions={0} | all-to-all | bytes 2097152 | tf_op jit(solution)/shard_map/all_to_all | solution.py:74
  (252 shorter events, 234.8 us)
Async XLA Ops:
  26.9 62.0 %all-to-all-start = ((bf16[256,3,2048]{0,1,2:T(4,128)(2,1)}), bf16[256,3,2048]{0,1,2:T(4,128)(2,1)}, u32[]{:S(2)}, u32[]{:S(2)}) async-start(bf16[256,3,2048]{0,1,2:T(4,128)(2,1)} %copy.40), calls=%async_computation | async-start | bytes 8388608 | tf_op jit(solution)/shard_map/all_to_all | solution.py:49
  36.2 253.9 %all-gather.2.cloned.1.call-start = ((), (), s32[]{:S(2)}) async-start(), calls=%async_computation.2 | async-start | bytes 18874368 | tf_op jit(solution)/shard_map/all_gather | solution.py:63
  110.2 4.5 copy-start
  140.5 1.2 copy-start.4
  140.5 1.2 copy-start.6
  163.6 1.1 copy-start.8
  163.6 1.1 copy-start.10
  186.3 0.6 copy-start.12
  186.3 0.6 copy-start.14
  206.8 88.6 %copy-start.1 = (f32[4,2,512,64]{2,3,1,0:T(8,128)}, f32[4,2,512,64]{2,3,1,0:T(8,128)S(1)}, u32[]{:S(2)}) copy-start(f32[4,2,512,64]{2,3,1,0:T(8,128)S(1)} %get-tuple-element.419) | copy-start | bytes 3145732
  206.8 88.9 %copy-start.16 = (f32[4,2,512]{2,1,0:T(2,128)}, f32[4,2,512]{2,1,0:T(2,128)S(1)}, u32[]{:S(2)}) copy-start(f32[4,2,512]{2,1,0:T(2,128)S(1)} %get-tuple-element.414) | copy-start | bytes 49156
  206.8 88.9 %copy-start.18 = (f32[4,2,512]{2,1,0:T(2,128)}, f32[4,2,512]{2,1,0:T(2,128)S(1)}, u32[]{:S(2)}) copy-start(f32[4,2,512]{2,1,0:T(2,128)S(1)} %get-tuple-element.424) | copy-start | bytes 49156
  339.0 1.0 copy-start.2
  342.7 21.6 %copy-start.5 = (f32[4,2,512]{2,1,0:T(2,128)S(1)}, f32[4,2,512]{2,1,0:T(2,128)}, u32[]{:S(2)}) copy-start(f32[4,2,512]{2,1,0:T(2,128)} %copy-done.4) | copy-start | bytes 49156
  342.7 21.6 %copy-start.7 = (f32[4,2,512]{2,1,0:T(2,128)S(1)}, f32[4,2,512]{2,1,0:T(2,128)}, u32[]{:S(2)}) copy-start(f32[4,2,512]{2,1,0:T(2,128)} %copy-done.6) | copy-start | bytes 49156
  342.8 21.6 %copy-start.9 = (f32[4,2,512]{2,1,0:T(2,128)S(1)}, f32[4,2,512]{2,1,0:T(2,128)}, u32[]{:S(2)}) copy-start(f32[4,2,512]{2,1,0:T(2,128)} %copy-done.8) | copy-start | bytes 49156
  342.8 21.6 %copy-start.11 = (f32[4,2,512]{2,1,0:T(2,128)S(1)}, f32[4,2,512]{2,1,0:T(2,128)}, u32[]{:S(2)}) copy-start(f32[4,2,512]{2,1,0:T(2,128)} %copy-done.10) | copy-start | bytes 49156
  388.4 1.0 copy-start.3
  414.0 20.0 %copy-start.13 = (f32[4,2,512]{2,1,0:T(2,128)S(1)}, f32[4,2,512]{2,1,0:T(2,128)}, u32[]{:S(2)}) copy-start(f32[4,2,512]{2,1,0:T(2,128)} %copy-done.12) | copy-start | bytes 49156
  414.0 20.0 %copy-start.15 = (f32[4,2,512]{2,1,0:T(2,128)S(1)}, f32[4,2,512]{2,1,0:T(2,128)}, u32[]{:S(2)}) copy-start(f32[4,2,512]{2,1,0:T(2,128)} %copy-done.14) | copy-start | bytes 49156
  414.0 20.0 %copy-start.17 = (f32[4,2,512]{2,1,0:T(2,128)S(1)}, f32[4,2,512]{2,1,0:T(2,128)}, u32[]{:S(2)}) copy-start(f32[4,2,512]{2,1,0:T(2,128)} %copy-done.16) | copy-start | bytes 49156
  414.0 20.0 %copy-start.19 = (f32[4,2,512]{2,1,0:T(2,128)S(1)}, f32[4,2,512]{2,1,0:T(2,128)}, u32[]{:S(2)}) copy-start(f32[4,2,512]{2,1,0:T(2,128)} %copy-done.18) | copy-start | bytes 49156
Sparse Core Ops, SparseCore 0:
  112.6 177.4 all-gather.1
where the time goes:
time: 477 us; the launch traced here: 471 us
  matrix products  142 us (30%)
  waiting for transfers between devices  136 us (29%)
  local copies, waits for them, and re-layouts  72 us (15%)
  other arithmetic  71.9 us (15%)
  blocking collectives  23.8 us (5%)
  between operations  14.1 us (3%)
  starting transfers between devices  9.34 us (2%)
    dot_general x40, matrix products, one_tile(): jnp.einsum('hqk,khd->hqd', probs, values, preferred_element_type=jnp.floa...  87 us
    all_gather x1, waiting for transfers between devices, on_device(): gathered = lax.all_gather(pairs, 'blk', axis=0, tiled=True)  83.2 us
    reduce_sum x40, other arithmetic, one_tile(): total = jnp.sum(probs.astype(jnp.float32), axis=-1)  65.6 us
    dot_general x40, matrix products, one_tile(): jnp.einsum('qhd,khd->hqk', query_tile, keys, preferred_element_type=jnp.f...  55.4 us
    all_to_all x1, waiting for transfers between devices, on_device(): lax.all_to_all(shaped, 'head', split_axis=2, concat_axis=0, tiled=True)  52.6 us
    all_to_all x1, blocking collectives, on_device(): lax.all_to_all(outputs, 'head', split_axis=0, concat_axis=1, tiled=True)  23.8 us
    reshape x1, local copies, waits for them, and re-layouts, on_device(): shaped = qkv.reshape(rows, 3, heads_cols)  17.2 us
  transfers between devices with their start and end apart: 2, of which 2 were waited for; matrix products, arithmetic and copies ran while one was open for 20% of the time, Pallas kernels for 0%

commit v1 on v0

--- a/solution.py
+++ b/solution.py
@@ -60,7 +60,10 @@
             partials[j].append(attend(queries[j], pairs[j]))
             partials[j].append(attend(queries[j], pairs[j ^ 1 << 0]))
 
-    gathered = lax.all_gather(pairs, "blk", axis=0, tiled=True)
+    devices = lax.axis_size("blk")
+    blocks = jnp.stack([pairs for _ in range(devices)])
+    blocks = lax.all_to_all(blocks, "blk", split_axis=0, concat_axis=0)
+    gathered = jnp.concatenate(blocks, axis=0)
     mine = lax.axis_index("blk")
     for bit in range(device_bits):
         for j in range(BLK_DEV):

time: 477 us -> 554 us (1.16)
  the two profiles are of different devices: /device:TPU:1 before, /device:TPU:6 now
where the time goes in v1:
time: 554 us; the launch traced here: 549 us
  waiting for transfers between devices  210 us (38%)
  matrix products  141 us (25%)
  local copies, waits for them, and re-layouts  78.8 us (14%)
  other arithmetic  72 us (13%)
  blocking collectives  30.2 us (5%)
  starting transfers between devices  15.1 us (3%)
    all_to_all x1, waiting for transfers between devices, on_device(): blocks = lax.all_to_all(blocks, 'blk', split_axis=0, concat_axis=0)  158 us
    dot_general x40, matrix products, one_tile(): jnp.einsum('hqk,khd->hqd', probs, values, preferred_element_type=jnp.floa...  85.2 us
    reduce_sum x40, other arithmetic, one_tile(): total = jnp.sum(probs.astype(jnp.float32), axis=-1)  65.6 us
    dot_general x40, matrix products, one_tile(): jnp.einsum('qhd,khd->hqk', query_tile, keys, preferred_element_type=jnp.f...  55.4 us
    all_to_all x1, waiting for transfers between devices, on_device(): lax.all_to_all(shaped, 'head', split_axis=2, concat_axis=0, tiled=True)  52.3 us
    all_to_all x1, blocking collectives, on_device(): lax.all_to_all(outputs, 'head', split_axis=0, concat_axis=1, tiled=True)  30.2 us
    reshape x1, local copies, waits for them, and re-layouts, on_device(): shaped = qkv.reshape(rows, 3, heads_cols)  17.1 us
    unnamed x50, local copies, waits for them, and re-layouts  12.1 us
  transfers between devices with their start and end apart: 2, of which 2 were waited for; matrix products, arithmetic and copies ran while one was open for 17% of the time, Pallas kernels for 0%

profile of v1, /device:TPU:6, one launch (start us, length us, event | category | flops | bytes accessed | tf_op | source)
XLA Modules:
  0.0 549.3 jit_solution(2398714621856427508)
XLA Ops:
  3.2 17.1 %copy.42 = bf16[256,3,2048]{0,1,2:T(4,128)(2,1)} copy(bf16[256,3,2048]{0,2,1:T(8,128)(2,1)S(1)} %bitcast.367) | data formatting | bytes 6291456 | tf_op jit(solution)/shard_map/reshape | solution.py:48
  20.3 8.5 %all-to-all-start = ((bf16[256,3,2048]{0,1,2:T(4,128)(2,1)}), bf16[256,3,2048]{0,1,2:T(4,128)(2,1)}, u32[]{:S(2)}, u32[]{:S(2)}) async-start(bf16[256,3,2048]{0,1,2:T(4,128)(2,1)} %copy.42), calls=%async_computation | async-start | bytes 8388608 | tf_op jit(solution)/shard_map/all_to_all | solution.py:49
  28.8 52.3 %all-to-all-done = bf16[256,3,2048]{0,1,2:T(4,128)(2,1)} async-done(((bf16[256,3,2048]{0,1,2:T(4,128)(2,1)}), bf16[256,3,2048]{0,1,2:T(4,128)(2,1)}, u32[]{:S(2)}, u32[]{:S(2)}) %all-to-all-start) | async-done | bytes 3145760 | tf_op jit(solution)/shard_map/all_to_all | solution.py:49
  83.8 3.5 copy.44
  87.3 3.8 reshape.52
  92.9 5.2 slice_reduce_fusion.1
  98.1 4.2 fusion.62
  103.2 6.0 %stack.2 = bf16[8,2,2048,2,2,64]{2,5,4,3,1,0:T(8,128)(2,1)} broadcast(bf16[2,2048,2,2,64]{1,4,3,2,0:T(8,128)(2,1)S(1)} %copy.45), dimensions={1,2,3,4,5} | broadcast | bytes 18874368 | tf_op jit(solution)/shard_map/stack | solution.py:64
  109.2 6.6 %all-to-all-start.1 = ((bf16[8,2,2048,2,2,64]{2,5,4,3,1,0:T(8,128)(2,1)}), bf16[8,2,2048,2,2,64]{2,5,4,3,1,0:T(8,128)(2,1)}, u32[]{:S(2)}, u32[]{:S(2)}) async-start(bf16[8,2,2048,2,2,64]{2,5,4,3,1,0:T(8,128)(2,1)} %stack.2), calls=%async_computation.1 | async-start | bytes 33554432 | tf_op jit(solution)/shard_map/all_to_all | solution.py:65
  115.9 3.8 copy_bitcast_fusion
  120.0 19.9 %while.143 = (s32[]{:T(128)}, f32[4,2,512]{2,1,0:T(2,128)S(1)}, f32[4,2,512]{2,1,0:T(2,128)S(1)}, f32[4,2,512,64]{2,3,1,0:T(8,128)S(1)}, bf16[4,512,2,64]{1,3,2,...) while((s32[]{:T(128)}, f32[4,2,512]{2,1,0:T(2,128)S(1)}, ...), condition=%wide.region_15.16_spmd, body=%wide.region_12.15_spmd.sunk | while | flops 557840384 | bytes 26640480 | solution.py:28
  143.3 21.6 %while.144 = (s32[]{:T(128)}, f32[4,2,512]{2,1,0:T(2,128)S(1)}, f32[4,2,512]{2,1,0:T(2,128)S(1)}, f32[4,2,512,64]{2,3,1,0:T(8,128)}, bf16[4,512,2,64]{1,3,2,0:T(...) while((s32[]{:T(128)}, f32[4,2,512]{2,1,0:T(2,128)S(1)}, ...), condition=%wide.region_19.20_spmd, body=%wide.region_16.19_spmd.sunk | while | flops 557840384 | bytes 26640988 | solution.py:28
  167.7 21.6 %while.148 = (s32[]{:T(128)}, f32[4,2,512]{2,1,0:T(2,128)S(1)}, f32[4,2,512]{2,1,0:T(2,128)S(1)}, f32[4,2,512,64]{2,3,1,0:T(8,128)}, bf16[4,512,2,64]{1,3,2,0:T(...) while((s32[]{:T(128)}, f32[4,2,512]{2,1,0:T(2,128)S(1)}, ...), condition=%wide.region_35.36_spmd, body=%wide.region_32.35_spmd.sunk | while | flops 557840384 | bytes 26640988 | solution.py:28
  190.0 20.1 %while.149 = (s32[]{:T(128)}, f32[4,2,512]{2,1,0:T(2,128)S(1)}, f32[4,2,512]{2,1,0:T(2,128)S(1)}, f32[4,2,512,64]{2,3,1,0:T(8,128)S(1)}, bf16[4,512,2,64]{1,3,2,...) while((s32[]{:T(128)}, f32[4,2,512]{2,1,0:T(2,128)S(1)}, ...), condition=%wide.region_39.40_spmd, body=%wide.region_36.39_spmd.sunk | while | flops 557840384 | bytes 26640480 | solution.py:28
  210.1 157.9 %all-to-all-done.1 = bf16[8,2,2048,2,2,64]{2,5,4,3,1,0:T(8,128)(2,1)} async-done(((bf16[8,2,2048,2,2,64]{2,5,4,3,1,0:T(8,128)(2,1)}), bf16[8,2,2048,2,2,64]{2,5,4,3,1,0:T(8,128)(2,1)}, u32[]{:S(2)}, u32[]{:S(2)}) %all-to-all-start.1) | async-done | bytes 16777248 | tf_op jit(solution)/shard_map/all_to_all | solution.py:65
  368.0 5.2 dynamic-slice_bitcast_fusion.5
  374.7 21.7 %while.140 = (s32[]{:T(128)}, f32[4,2,512]{2,1,0:T(2,128)S(1)}, f32[4,2,512]{2,1,0:T(2,128)S(1)}, f32[4,2,512,64]{2,3,1,0:T(8,128)}, bf16[4,512,2,64]{1,3,2,0:T(...) while((s32[]{:T(128)}, f32[4,2,512]{2,1,0:T(2,128)S(1)}, ...), condition=%wide.region_3.4_spmd, body=%wide.region_0.3_spmd.sunk | while | flops 557840384 | bytes 26640988 | solution.py:28
  396.5 19.9 %while.141 = (s32[]{:T(128)}, f32[4,2,512]{2,1,0:T(2,128)S(1)}, f32[4,2,512]{2,1,0:T(2,128)S(1)}, f32[4,2,512,64]{2,3,1,0:T(8,128)S(1)}, bf16[4,512,2,64]{1,3,2,...) while((s32[]{:T(128)}, f32[4,2,512]{2,1,0:T(2,128)S(1)}, ...), condition=%wide.region_7.8_spmd, body=%wide.region_4.7_spmd.sunk | while | flops 557840384 | bytes 26640480 | solution.py:28
  420.2 22.0 %while.142 = (s32[]{:T(128)}, f32[4,2,512]{2,1,0:T(2,128)S(1)}, f32[4,2,512]{2,1,0:T(2,128)S(1)}, f32[4,2,512,64]{2,3,1,0:T(8,128)}, bf16[4,512,2,64]{1,3,2,0:T(...) while((s32[]{:T(128)}, f32[4,2,512]{2,1,0:T(2,128)S(1)}, ...), condition=%wide.region_11.12_spmd, body=%wide.region_8.11_spmd.sunk | while | flops 557840384 | bytes 26640988 | solution.py:28
  442.3 3.3 fusion.60
  447.0 19.9 %while.145 = (s32[]{:T(128)}, f32[4,2,512]{2,1,0:T(2,128)S(1)}, f32[4,2,512]{2,1,0:T(2,128)S(1)}, f32[4,2,512,64]{2,3,1,0:T(8,128)S(1)}, bf16[4,512,2,64]{1,3,2,...) while((s32[]{:T(128)}, f32[4,2,512]{2,1,0:T(2,128)S(1)}, ...), condition=%wide.region_23.24_spmd, body=%wide.region_20.23_spmd.sunk | while | flops 557840384 | bytes 26640480 | solution.py:28
  470.7 21.6 %while.146 = (s32[]{:T(128)}, f32[4,2,512]{2,1,0:T(2,128)S(1)}, f32[4,2,512]{2,1,0:T(2,128)S(1)}, f32[4,2,512,64]{2,3,1,0:T(8,128)}, bf16[4,512,2,64]{1,3,2,0:T(...) while((s32[]{:T(128)}, f32[4,2,512]{2,1,0:T(2,128)S(1)}, ...), condition=%wide.region_27.28_spmd, body=%wide.region_24.27_spmd.sunk | while | flops 557840384 | bytes 26640988 | solution.py:28
  492.5 20.1 %while.147 = (s32[]{:T(128)}, f32[4,2,512]{2,1,0:T(2,128)S(1)}, f32[4,2,512]{2,1,0:T(2,128)S(1)}, f32[4,2,512,64]{2,3,1,0:T(8,128)S(1)}, bf16[4,512,2,64]{1,3,2,...) while((s32[]{:T(128)}, f32[4,2,512]{2,1,0:T(2,128)S(1)}, ...), condition=%wide.region_31.32_spmd, body=%wide.region_28.31_spmd.sunk | while | flops 557840384 | bytes 26640480 | solution.py:28
  517.0 30.2 %all_to_all.36 = bf16[16,256,128]{2,1,0:T(8,128)(2,1)S(1)} all-to-all(bf16[16,256,128]{2,1,0:T(8,128)(2,1)S(1)} %bitcast.368), channel_id=1, replica_groups=mesh['blk'=8,'head'=16] {'head'}, dimensions={0} | all-to-all | bytes 2097152 | tf_op jit(solution)/shard_map/all_to_all | solution.py:77
  (258 shorter events, 239.2 us)
Async XLA Ops:
  20.3 60.8 %all-to-all-start = ((bf16[256,3,2048]{0,1,2:T(4,128)(2,1)}), bf16[256,3,2048]{0,1,2:T(4,128)(2,1)}, u32[]{:S(2)}, u32[]{:S(2)}) async-start(bf16[256,3,2048]{0,1,2:T(4,128)(2,1)} %copy.42), calls=%async_computation | async-start | bytes 8388608 | tf_op jit(solution)/shard_map/all_to_all | solution.py:49
  109.2 6.6 %copy-start.6 = (bf16[2048,2,64]{0,2,1:T(8,128)(2,1)S(1)}, bf16[2048,2,64]{0,2,1:T(8,128)(2,1)}, u32[]{:S(2)}) copy-start(bf16[2048,2,64]{0,2,1:T(8,128)(2,1)} %get-tuple-element.670) | copy-start | bytes 1572868
  109.2 6.7 %copy-start = (bf16[1,2048,2,2,64]{1,0,4,3,2:T(2,128)(2,1)S(1)}, bf16[1,2048,2,2,64]{1,0,4,3,2:T(2,128)(2,1)}, u32[]{:S(2)}) copy-start(bf16[1,2048,2,2,64]{1,0,4,3,2:T(2,128)(2,1)} %get-tuple-element.870) | copy-start | bytes 3145732
  109.2 258.8 %all-to-all-start.1 = ((bf16[8,2,2048,2,2,64]{2,5,4,3,1,0:T(8,128)(2,1)}), bf16[8,2,2048,2,2,64]{2,5,4,3,1,0:T(8,128)(2,1)}, u32[]{:S(2)}, u32[]{:S(2)}) async-start(bf16[8,2,2048,2,2,64]{2,5,4,3,1,0:T(8,128)(2,1)} %stack.2), calls=%async_computation.1 | async-start | bytes 33554432 | tf_op jit(solution)/shard_map/all_to_all | solution.py:65
  139.9 1.0 copy-start.1
  140.9 2.4 copy-start.7
  140.9 2.4 copy-start.9
  164.9 0.6 copy-start.13
  189.3 0.6 copy-start.15
  189.3 0.6 copy-start.17
  210.1 163.2 %copy-start.2 = (f32[4,2,512,64]{2,3,1,0:T(8,128)}, f32[4,2,512,64]{2,3,1,0:T(8,128)S(1)}, u32[]{:S(2)}) copy-start(f32[4,2,512,64]{2,3,1,0:T(8,128)S(1)} %get-tuple-element.419) | copy-start | bytes 3145732
  210.1 163.5 %copy-start.19 = (f32[4,2,512]{2,1,0:T(2,128)}, f32[4,2,512]{2,1,0:T(2,128)S(1)}, u32[]{:S(2)}) copy-start(f32[4,2,512]{2,1,0:T(2,128)S(1)} %get-tuple-element.414) | copy-start | bytes 49156
  210.1 163.5 %copy-start.21 = (f32[4,2,512]{2,1,0:T(2,128)}, f32[4,2,512]{2,1,0:T(2,128)S(1)}, u32[]{:S(2)}) copy-start(f32[4,2,512]{2,1,0:T(2,128)S(1)} %get-tuple-element.424) | copy-start | bytes 49156
  416.4 1.0 copy-start.3
  420.2 22.1 %copy-start.8 = (f32[4,2,512]{2,1,0:T(2,128)S(1)}, f32[4,2,512]{2,1,0:T(2,128)}, u32[]{:S(2)}) copy-start(f32[4,2,512]{2,1,0:T(2,128)} %copy-done.7) | copy-start | bytes 49156
  420.2 22.1 %copy-start.10 = (f32[4,2,512]{2,1,0:T(2,128)S(1)}, f32[4,2,512]{2,1,0:T(2,128)}, u32[]{:S(2)}) copy-start(f32[4,2,512]{2,1,0:T(2,128)} %copy-done.9) | copy-start | bytes 49156
  420.2 22.1 %copy-start.12 = (f32[4,2,512]{2,1,0:T(2,128)S(1)}, f32[4,2,512]{2,1,0:T(2,128)}, u32[]{:S(2)}) copy-start(f32[4,2,512]{2,1,0:T(2,128)} %copy-done.11) | copy-start | bytes 49156
  420.2 22.1 %copy-start.14 = (f32[4,2,512]{2,1,0:T(2,128)S(1)}, f32[4,2,512]{2,1,0:T(2,128)}, u32[]{:S(2)}) copy-start(f32[4,2,512]{2,1,0:T(2,128)} %copy-done.13) | copy-start | bytes 49156
  467.0 1.0 copy-start.4
  492.5 20.1 %copy-start.16 = (f32[4,2,512]{2,1,0:T(2,128)S(1)}, f32[4,2,512]{2,1,0:T(2,128)}, u32[]{:S(2)}) copy-start(f32[4,2,512]{2,1,0:T(2,128)} %copy-done.15) | copy-start | bytes 49156
  492.5 20.1 %copy-start.18 = (f32[4,2,512]{2,1,0:T(2,128)S(1)}, f32[4,2,512]{2,1,0:T(2,128)}, u32[]{:S(2)}) copy-start(f32[4,2,512]{2,1,0:T(2,128)} %copy-done.17) | copy-start | bytes 49156
  492.5 20.1 %copy-start.20 = (f32[4,2,512]{2,1,0:T(2,128)S(1)}, f32[4,2,512]{2,1,0:T(2,128)}, u32[]{:S(2)}) copy-start(f32[4,2,512]{2,1,0:T(2,128)} %copy-done.19) | copy-start | bytes 49156
  492.5 20.1 %copy-start.22 = (f32[4,2,512]{2,1,0:T(2,128)S(1)}, f32[4,2,512]{2,1,0:T(2,128)}, u32[]{:S(2)}) copy-start(f32[4,2,512]{2,1,0:T(2,128)} %copy-done.21) | copy-start | bytes 49156
  512.6 3.6 copy-start.5
  (1 other events, 0.6 us)
